TPU v7x, 32 devices: a whole 2x2x4 slice. The times are simulated.
32 devices in a mesh: bead: 4 (over x, core), slab: 8 (over z, y).
Axes of the slice: x: 2, y: 2, z: 4, core: 2. Of those that a mesh axis runs over, the one named last changes fastest.
Arguments:
- positions: float32 [16, 3, 8192], P('bead', None, 'slab'), may hold values from -0.4 to 16.4, as said below
- velocities: float32 [16, 3, 8192], P('bead', None, 'slab'), may hold values from -5 to 5
- masses: float32 [8192], P('slab'), may hold values from 1 to 16
- amplitudes: float32 [8192], P('slab'), may hold values from 0.15 to 0.6
- charges: float32 [8192], P('slab'), may hold values from -1.2 to 1.2
Outputs:
- moved: float32 [16, 3, 8192], P('bead', None, 'slab')
- final_velocities: float32 [16, 3, 8192], P('bead', None, 'slab')
Inputs may be any that keep to these rules, and one draw needn't show every extreme that they name: `positions`: atom n's beads lie within 0.4 of its cell: plane n // 512 spans first coordinates from its index to its index plus one, and cell (n % 512) // 128 = 2 a + e of that plane spans second coordinates a to a + 1 and third coordinates e to e + 1.
All inputs are finite; a program needn't handle non-finite values.
Results may differ from a plain program's by a relative error of at most 0.0003.
Values sent between devices are 32-bit elements; how exact they have to be, the bound alone decides.
A program may use at most 64 MiB of HBM per device.

v0:
```python
import math

import jax
import jax.numpy as jnp
import numpy as np
from jax import lax
from jax.experimental import pallas as pl
from jax.experimental.pallas import tpu as pltpu
from jax.sharding import PartitionSpec as P

INNER_STEPS = 2
OUTER_STEPS = 2
PLANE_ATOMS = 512

time_step = 0.05
spring_rate = 25.0
near_scale = 4.0
far_scale = 2.0

MESH = pl.DeviceIdType.MESH
F32 = jnp.float32
BF16 = jnp.bfloat16
PA = PLANE_ATOMS
PHASES = INNER_STEPS * OUTER_STEPS + 1
EVENTS = OUTER_STEPS + 1
FEATURES = 64


def contraction(bead_count, small_count):
    bead_place = np.arange(bead_count, dtype=np.float64) / bead_count
    small_place = np.arange(small_count, dtype=np.float64) / small_count
    phase = 2.0 * np.pi * (bead_place[None, :] - small_place[:, None])
    modes = np.arange(1, small_count // 2, dtype=np.float64)
    total = 1.0 + np.cos(0.5 * small_count * phase)
    total = total + 2.0 * np.sum(np.cos(modes[:, None, None] * phase[None]), axis=0)
    return (total / bead_count).astype(np.float32)


def rows_of(width):
    return lax.broadcasted_iota(jnp.int32, (8, width), 0)


def cut(x):
    high = x.astype(BF16).astype(F32)
    rest = x - high
    mid = rest.astype(BF16).astype(F32)
    low = (rest - mid).astype(BF16).astype(F32)
    return high, mid, low


def scaled(x, first_centre, rate):
    quarter = rows_of(x.shape[1]) & 3
    centre = jnp.where(quarter == 0, first_centre, jnp.where(quarter == 3, 0.0, 1.0))
    return (x - centre) * rate


def source_features(z, share):
    quarter = rows_of(z.shape[1]) & 3
    square = 0.5 * z * z
    norm = pltpu.roll(square, 1, 0) + pltpu.roll(square, 2, 0) + pltpu.roll(square, 3, 0)
    high, mid, low = cut(jnp.where(quarter == 3, norm, z))
    one = jnp.ones_like(z)
    features = jnp.concatenate([high, high, mid, mid, high, low, one, jnp.zeros_like(z)], axis=0)
    weighted = share * jnp.where(quarter == 3, 1.0, z)
    first, second, _ = cut(weighted)
    return features.T.astype(BF16), jnp.concatenate([first, second], axis=0).astype(BF16)


def target_features(z):
    quarter = rows_of(z.shape[1]) & 3
    square = 0.5 * z * z
    norm = pltpu.roll(square, 1, 0) + pltpu.roll(square, 2, 0) + pltpu.roll(square, 3, 0)
    high, mid, low = cut(jnp.where(quarter == 3, norm, z))
    flat = quarter == 3
    own = jnp.where(
        flat,
        -high,
        jnp.where(quarter == 2, -pltpu.roll(mid, 7, 0), jnp.where(quarter == 1, -pltpu.roll(low, 6, 0), 0.0)),
    )
    high = jnp.where(flat, -1.0, high)
    mid = jnp.where(flat, 0.0, mid)
    low = jnp.where(flat, 0.0, low)
    return [high, mid, high, mid, low, high, own, jnp.zeros_like(z)]


def masked(groups, half):
    keep = (rows_of(groups[0].shape[1]) >> 2) == half
    return jnp.concatenate([jnp.where(keep, g, 0.0) for g in groups], axis=0).astype(BF16)


def block_sums(sources, weighted, targets, pieces):
    weight = jnp.exp2(jnp.dot(sources, targets, preferred_element_type=F32))
    high = weight.astype(BF16)
    total = jnp.dot(weighted, high, preferred_element_type=F32)
    if pieces == 2:
        rest = (weight - high.astype(F32)).astype(BF16)
        total = total + jnp.dot(weighted, rest, preferred_element_type=F32)
    return total


def forces_of(z, sums):
    quarter = rows_of(z.shape[1]) & 3
    plain = jnp.where(quarter == 3, sums, 0.0)
    spread = pltpu.roll(plain, 7, 0) + pltpu.roll(plain, 6, 0) + pltpu.roll(plain, 5, 0)
    return jnp.where(quarter == 3, 0.0, z * spread - sums)


def kernel(
    nb, ns, planes_total,
    table, pos, vel, mass, amp, chg,
    moved, final,
    X, V, AF, AS, prm, prm_l, prm_r, halo_l, halo_r, ring_p, ring_n,
    part_s, part_r, Y, y_l, y_r, far_s, far_r,
    nST, nXS, nT, nG, fST, fXS, fT, fG,
    prm_ss, prm_rs, halo_ss, halo_rs, ring_ss, ring_rs, part_ss, part_rs, y_ss, y_rs, far_ss, far_rs,
):
    me_b = lax.axis_index("bead")
    me_s = lax.axis_index("slab")
    left = (me_b, lax.rem(me_s + ns - 1, ns))
    right = (me_b, lax.rem(me_s + 1, ns))
    prev = (lax.rem(me_b + nb - 1, nb), me_s)
    after = (lax.rem(me_b + 1, nb), me_s)
    pairs = X.shape[1]
    beads_here = 2 * pairs
    atoms = X.shape[3]
    first_bead = me_b * beads_here

    def remote(src, dst, ss, rs, to):
        return pltpu.make_async_remote_copy(
            src_ref=src, dst_ref=dst, send_sem=ss, recv_sem=rs, device_id=to, device_id_type=MESH
        )

    barrier = pltpu.get_barrier_semaphore()
    pl.semaphore_signal(barrier, inc=1, device_id=left, device_id_type=MESH)
    pl.semaphore_signal(barrier, inc=1, device_id=right, device_id_type=MESH)
    for d in range(1, nb):
        other = (lax.rem(me_b + d, nb), me_s)
        pl.semaphore_signal(barrier, inc=1, device_id=other, device_id_type=MESH)

    X[0] = jnp.zeros((pairs, 8, atoms), F32)
    V[...] = jnp.zeros_like(V)
    for b in range(beads_here):
        p, r = b // 2, 4 * (b % 2)
        X[0, p, r:r + 3, :] = pos[b]
        V[p, r:r + 3, :] = vel[b]
    prm[...] = jnp.zeros_like(prm)
    for t in range(2):
        lanes = slice(t * PA, (t + 1) * PA)
        prm[t:t + 1, :] = amp[:, lanes]
        prm[2 + t:3 + t, :] = chg[:, lanes]

    pl.semaphore_wait(barrier, nb + 1)

    prm_copies = [
        remote(prm, prm_r, prm_ss.at[0], prm_rs.at[0], left),
        remote(prm, prm_l, prm_ss.at[1], prm_rs.at[1], right),
    ]
    for copy in prm_copies:
        copy.start()

    centre = (me_s * 2).astype(F32) + 1.0
    span = float(planes_total)
    centre_l = centre + jnp.where(me_s == 0, span, 0.0)
    centre_r = centre - jnp.where(me_s == ns - 1, span, 0.0)
    near_rate = math.sqrt(near_scale / math.log(2.0))
    far_rate = math.sqrt(far_scale / math.log(2.0))

    inverse = 1.0 / mass[...]

    def halo_copies(k):
        return [
            remote(X.at[k, :, :, pl.ds(0, PA)], halo_r.at[k], halo_ss.at[k, 0], halo_rs.at[k, 0], left),
            remote(X.at[k, :, :, pl.ds(atoms - PA, PA)], halo_l.at[k], halo_ss.at[k, 1], halo_rs.at[k, 1], right),
        ]

    def ring_copies(k):
        return [
            remote(X.at[k, pairs - 1], ring_p.at[k], ring_ss.at[k, 0], ring_rs.at[k, 0], after),
            remote(X.at[k, 0], ring_n.at[k], ring_ss.at[k, 1], ring_rs.at[k, 1], prev),
        ]

    def spoke_copies(src, dst, ss, rs, e):
        return [
            remote(src(d), dst.at[e, d], ss.at[e, d], rs.at[e, d], (lax.rem(me_b + d, nb), me_s))
            for d in range(1, nb)
        ]

    def part_copies(e):
        return spoke_copies(lambda d: part_s.at[e, d], part_r, part_ss, part_rs, e)

    def far_copies(e):
        return spoke_copies(lambda d: far_s.at[e], far_r, far_ss, far_rs, e)

    def y_copies(e):
        return [
            remote(Y.at[e], y_r.at[e], y_ss.at[e, 0], y_rs.at[e, 0], left),
            remote(Y.at[e], y_l.at[e], y_ss.at[e, 1], y_rs.at[e, 1], right),
        ]

    low_rows = rows_of(PA) < 4

    def partial_of(k, c):
        total = None
        for p in range(pairs):
            first = table[c, first_bead + 2 * p]
            second = table[c, first_bead + 2 * p + 1]
            term = jnp.where(rows_of(atoms) < 4, first, second) * X[k, p]
            total = term if total is None else total + term
        total = total + pltpu.roll(total, 4, 0)
        return jnp.where(low_rows, total[:, :PA], total[:, PA:])

    def far_halves(tile):
        first = jnp.where(low_rows, tile, 0.0)
        second = jnp.where(low_rows, pltpu.roll(tile, 4, 0), 0.0)
        return first, second

    def near_block(p, t, q):
        sources, weighted = nST[p, q], nXS[p, q]
        first = block_sums(sources, weighted, nT[p, t, 0], 1)
        second = block_sums(sources, weighted, nT[p, t, 1], 1)
        both = jnp.where(low_rows, first[:8] + first[8:], second[:8] + second[8:])
        nG[p, t] += both

    def far_block(t, q):
        sums = block_sums(fST[q], fXS[q], fT[t], 2)
        fG[t] += sums[:8] + sums[8:]

    def phase(k, carry):
        slow_turn = lax.rem(k, INNER_STEPS) == 0
        e = k // INNER_STEPS
        for copy in halo_copies(k):
            copy.start()

        @pl.when(slow_turn)
        def _():
            for d in range(1, nb):
                part_s[e, d] = partial_of(k, lax.rem(me_b + d, nb))
            for copy in part_copies(e):
                copy.start()

        for copy in ring_copies(k):
            copy.start()

        for p in range(pairs):
            for t in range(2):
                lanes = slice(t * PA, (t + 1) * PA)
                z = scaled(X[k, p, :, lanes], centre, near_rate)
                nST[p, 1 + t], nXS[p, 1 + t] = source_features(z, amp[:, lanes])
                groups = target_features(z)
                nT[p, t, 0] = masked(groups, 0)
                nT[p, t, 1] = masked(groups, 1)
        nG[...] = jnp.zeros_like(nG)

        @pl.loop(0, pairs * 2)
        def _(n):
            p, t = n // 2, lax.rem(n, 2)
            near_block(p, t, 1)
            near_block(p, t, 2)

        @pl.when(k == 0)
        def _():
            for copy in prm_copies:
                copy.wait_recv()

        @pl.when(slow_turn)
        def _():
            total = partial_of(k, me_b)
            for d, copy in enumerate(part_copies(e)):
                copy.wait_recv()
                total = total + part_r[e, d + 1]
            Y[e] = total
            for copy in y_copies(e):
                copy.start()
            for t, half in enumerate(far_halves(total)):
                z = scaled(half, centre, far_rate)
                z = jnp.where(low_rows, z, 0.0)
                fST[2 + t], fXS[2 + t] = source_features(z, chg[:, t * PA:(t + 1) * PA])
                fT[t] = masked(target_features(z), 0)
            fG[...] = jnp.zeros_like(fG)

            @pl.loop(0, 2)
            def _(t):
                far_block(t, 2)
                far_block(t, 3)

            for copy in y_copies(e):
                copy.wait_recv()
            for base, tile, shares, middle in ((0, y_l, prm_l, centre_l), (4, y_r, prm_r, centre_r)):
                for t, half in enumerate(far_halves(tile[e])):
                    z = scaled(half, middle, far_rate)
                    z = jnp.where(low_rows, z, 0.0)
                    fST[base + t], fXS[base + t] = source_features(z, shares[2 + t:3 + t, :])

            @pl.loop(0, 2)
            def _(t):
                far_block(t, 1)
                far_block(t, 4)
                far_block(t, 5 * t)

            halves = []
            for t in range(2):
                lanes = slice(t * PA, (t + 1) * PA)
                z = scaled(far_halves(total)[t], centre, far_rate)
                coefficient = chg[:, lanes] * (far_scale / far_rate)
                halves.append(coefficient * forces_of(z, fG[t]))
            far_s[e] = jnp.where(low_rows, halves[0], pltpu.roll(halves[1], 4, 0))
            for copy in far_copies(e):
                copy.start()

        for copy in halo_copies(k):
            copy.wait_recv()
        for p in range(pairs):
            z = scaled(halo_l[k, p], centre_l, near_rate)
            nST[p, 0], nXS[p, 0] = source_features(z, prm_l[1:2, :])
            z = scaled(halo_r[k, p], centre_r, near_rate)
            nST[p, 3], nXS[p, 3] = source_features(z, prm_r[0:1, :])

        @pl.loop(0, pairs)
        def _(p):
            near_block(p, 0, 0)
            near_block(p, 1, 3)

        for copy in ring_copies(k):
            copy.wait_recv()
        upper = rows_of(atoms) < 4
        rolled = [pltpu.roll(X[k, p], 4, 0) for p in range(pairs)]
        before = [pltpu.roll(ring_p[k], 4, 0)] + rolled
        behind = rolled + [pltpu.roll(ring_n[k], 4, 0)]
        for p in range(pairs):
            springs = 2.0 * X[k, p] - rolled[p] - jnp.where(upper, before[p], behind[p + 1])
            AF[p] = -spring_rate * springs
            for t in range(2):
                lanes = slice(t * PA, (t + 1) * PA)
                z = scaled(X[k, p, :, lanes], centre, near_rate)
                coefficient = amp[:, lanes] * (near_scale / near_rate) * inverse[:, lanes]
                AF[p, :, lanes] += coefficient * forces_of(z, nG[p, t])

        edge = (k == 0) | (k == PHASES - 1)
        fast_step = jnp.where(edge, 0.5 * time_step, time_step)
        slow_step = jnp.where(edge, 0.5 * INNER_STEPS * time_step, INNER_STEPS * time_step)
        for p in range(pairs):
            V[p] += fast_step * AF[p]

        @pl.when(slow_turn)
        def _():
            for copy in far_copies(e):
                copy.wait_recv()
            ratio = float(beads_here)
            total = [[None, None] for _ in range(pairs)]
            for d in range(nb):
                tile = far_s[e] if d == 0 else far_r[e, d]
                c = lax.rem(me_b + nb - d, nb)
                turned = pltpu.roll(tile, 4, 0)
                doubled = (jnp.where(low_rows, tile, turned), jnp.where(low_rows, turned, tile))
                for p in range(pairs):
                    first = table[c, first_bead + 2 * p] * ratio
                    second = table[c, first_bead + 2 * p + 1] * ratio
                    level = jnp.where(low_rows, first, second)
                    for t in range(2):
                        term = level * doubled[t]
                        total[p][t] = term if d == 0 else total[p][t] + term
            for p in range(pairs):
                for t in range(2):
                    lanes = slice(t * PA, (t + 1) * PA)
                    V[p, :, lanes] += slow_step * inverse[:, lanes] * total[p][t]

        @pl.when(k < PHASES - 1)
        def _():
            for p in range(pairs):
                X[k + 1, p] = X[k, p] + time_step * V[p]

        return carry

    lax.fori_loop(0, PHASES, phase, 0)

    last = PHASES - 1
    for b in range(beads_here):
        p, r = b // 2, 4 * (b % 2)
        moved[b] = X[last, p, r:r + 3, :] - pos[b]
        final[b] = V[p, r:r + 3, :]

    for copy in prm_copies:
        copy.wait_send()

    @pl.loop(0, PHASES)
    def _(k):
        for copy in halo_copies(k) + ring_copies(k):
            copy.wait_send()

    @pl.loop(0, EVENTS)
    def _(e):
        for copy in part_copies(e) + y_copies(e) + far_copies(e):
            copy.wait_send()


def solution(mesh):
    nb, ns = mesh.shape["bead"], mesh.shape["slab"]

    def shards(positions, velocities, masses, amplitudes, charges):
        beads_here, _, atoms = positions.shape
        assert atoms == 2 * PA and beads_here % 2 == 0
        pairs = beads_here // 2
        table = jnp.asarray(contraction(beads_here * nb, nb))
        vmem = pl.BlockSpec(memory_space=pltpu.VMEM)
        out = jax.ShapeDtypeStruct(positions.shape, F32)
        V, D = pltpu.VMEM, pltpu.SemaphoreType.DMA
        tile = (8, PA)

        def body(*refs):
            kernel(nb, ns, 2 * ns, *refs)

        return pl.pallas_call(
            body,
            name="rod",
            out_shape=(out, out),
            in_specs=[pl.BlockSpec(memory_space=pltpu.SMEM)] + [vmem] * 5,
            out_specs=(vmem, vmem),
            scratch_shapes=[
                V((PHASES, pairs, 8, atoms), F32),
                V((pairs, 8, atoms), F32),
                V((pairs, 8, atoms), F32),
                V((pairs, 8, atoms), F32),
                V(tile, F32), V(tile, F32), V(tile, F32),
                V((PHASES, pairs) + tile, F32), V((PHASES, pairs) + tile, F32),
                V((PHASES, 8, atoms), F32), V((PHASES, 8, atoms), F32),
                V((EVENTS, nb) + tile, F32), V((EVENTS, nb) + tile, F32),
                V((EVENTS,) + tile, F32), V((EVENTS,) + tile, F32), V((EVENTS,) + tile, F32),
                V((EVENTS,) + tile, F32), V((EVENTS, nb) + tile, F32),
                V((pairs, 4, PA, FEATURES), BF16), V((pairs, 4, 16, PA), BF16),
                V((pairs, 2, 2, FEATURES, PA), BF16), V((pairs, 2) + tile, F32),
                V((6, PA, FEATURES), BF16), V((6, 16, PA), BF16),
                V((2, FEATURES, PA), BF16), V((2,) + tile, F32),
                D((2,)), D((2,)), D((PHASES, 2)), D((PHASES, 2)), D((PHASES, 2)), D((PHASES, 2)),
                D((EVENTS, nb)), D((EVENTS, nb)), D((EVENTS, 2)), D((EVENTS, 2)),
                D((EVENTS, nb)), D((EVENTS, nb)),
            ],
            compiler_params=pltpu.CompilerParams(collective_id=0, has_side_effects=True),
        )(table, positions, velocities, masses[None], amplitudes[None], charges[None])

    both = P("bead", None, "slab")
    return jax.shard_map(
        shards, mesh=mesh, in_specs=(both, both, P("slab"), P("slab"), P("slab")), out_specs=(both, both), check_vma=False
    )
```

profile of v0, /device:TPU:0, one launch (start us, length us, event | category | flops | bytes accessed | tf_op | source)
XLA Modules:
  0.0 73.2 jit_solution(979132882782661256)
XLA Ops:
  0.6 0.0 copy-start.1
  0.6 1.5 %copy.8.refs_1_ = f32[4,3,1024]{2,1,0:T(4,128)} copy(f32[4,3,1024]{2,0,1:T(4,128)} %param.6) | data formatting | bytes 98304 | tf_op args[0]
  2.1 0.0 copy-done.1
  2.1 0.7 copy.9.refs_2_
  2.8 68.2 %rod.1 = (f32[4,3,1024]{2,1,0:T(4,128)}, f32[4,3,1024]{2,1,0:T(4,128)}) custom-call(f32[4,16]{1,0:T(4,128)} %constant.2.clone.refs_0_, f32[4,3,1024]{2,1,0:T(4,128)} %copy.8.refs_1_, f32[4,3,1024]{2,1,0:T(4,128)} %copy.9.refs_2_, f32[1,1024]{1,0:T(1,128)} %bitcast.3, f32[1,1024]{1,0:T(1,128)} %bitcast.4, f32[1,1024]{1,0:T(1,128)} %bitcast.5), custom_call_target="tpu_custom_call" | custom-call | tf_op jit(solution)/shard_map/rod/pallas_call | solution.py:412
  71.0 0.0 copy-start
  71.0 1.5 %copy.10 = f32[4,3,1024]{2,0,1:T(4,128)} copy(f32[4,3,1024]{2,1,0:T(4,128)} %get-tuple-element.2) | data formatting | bytes 98304 | tf_op jit(solution)/shard_map/rod/pallas_call | solution.py:412
  72.5 0.0 copy-done
  72.5 0.7 copy.11
Async XLA Ops:
  0.6 1.5 %copy-start.1 = (f32[4,3,1024]{2,0,1:T(4,128)S(1)}, f32[4,3,1024]{2,0,1:T(4,128)}, u32[]{:S(2)}) copy-start(f32[4,3,1024]{2,0,1:T(4,128)} %param.7) | copy-start | bytes 147460
  71.0 1.5 %copy-start = (f32[4,3,1024]{2,1,0:T(4,128)S(1)}, f32[4,3,1024]{2,1,0:T(4,128)}, u32[]{:S(2)}) copy-start(f32[4,3,1024]{2,1,0:T(4,128)} %get-tuple-element.3) | copy-start | bytes 147460
where the time goes:
time: 73.4 us; the launch traced here: 73.2 us
  Pallas kernels  68.2 us (93%)
  local copies, waits for them, and re-layouts  4.31 us (6%)
    pallas_call x1, Pallas kernels, shards(): pl.pallas_call(body, name='rod', out_shape=(out, out), in_specs=[pl.Block...  68.2 us
    pallas_call x2, local copies, waits for them, and re-layouts, shards(): pl.pallas_call(body, name='rod', out_shape=(out, out), in_specs=[pl.Block...  2.18 us
    unnamed x6, local copies, waits for them, and re-layouts  2.13 us

commit v1 on v0

--- a/solution.py
+++ b/solution.py
@@ -24,6 +24,7 @@
 PHASES = INNER_STEPS * OUTER_STEPS + 1
 EVENTS = OUTER_STEPS + 1
 FEATURES = 64
+HALF = PA // 2
 
 
 def contraction(bead_count, small_count):
@@ -88,14 +89,49 @@
     return jnp.concatenate([jnp.where(keep, g, 0.0) for g in groups], axis=0).astype(BF16)
 
 
-def block_sums(sources, weighted, targets, pieces):
-    weight = jnp.exp2(jnp.dot(sources, targets, preferred_element_type=F32))
+def weighted_sum(weighted, weight, pieces, flip):
+    dims = (((1,), (1 if flip else 0,)), ((), ()))
     high = weight.astype(BF16)
-    total = jnp.dot(weighted, high, preferred_element_type=F32)
+    total = lax.dot_general(weighted, high, dims, preferred_element_type=F32)
     if pieces == 2:
         rest = (weight - high.astype(F32)).astype(BF16)
-        total = total + jnp.dot(weighted, rest, preferred_element_type=F32)
-    return total
+        total = total + lax.dot_general(weighted, rest, dims, preferred_element_type=F32)
+    return total[:8] + total[8:]
+
+
+def block_items(sources, weighted, targets, t, kind, others=None):
+    items = []
+    for h in range(2):
+        rows = slice(h * HALF, (h + 1) * HALF)
+        width = HALF if kind == "self" and h == 0 else PA
+        flips = None
+        if kind == "self" and h == 1:
+            flips = (weighted, HALF, (t, 1))
+        if kind == "cross":
+            flips = (others, PA, (1, h))
+        items.append((sources, rows, weighted, targets, width, t, flips))
+    return items
+
+
+def run_items(items, pieces, sums):
+    waiting = None
+    for item in list(items) + [None]:
+        exponent = None
+        if item is not None:
+            sources, rows, _, targets, width = item[:5]
+            exponent = jnp.dot(sources[rows, :], targets[:, :width], preferred_element_type=F32)
+        if waiting is not None:
+            (_, rows, weighted, _, width, t, flips), held = waiting
+            weight = jnp.exp2(held)
+            direct = weighted_sum(weighted[:, rows], weight, pieces, False)
+            for half in range(width // HALF):
+                part = direct[:, half * HALF:(half + 1) * HALF]
+                sums[t, half] = sums[t, half] + part if (t, half) in sums else part
+            if flips is not None:
+                shares, depth, key = flips
+                part = weighted_sum(shares[:, :depth], weight[:, :depth], pieces, True)
+                sums[key] = sums[key] + part if key in sums else part
+        waiting = (item, exponent)
 
 
 def forces_of(z, sums):
@@ -141,8 +177,9 @@
     V[...] = jnp.zeros_like(V)
     for b in range(beads_here):
         p, r = b // 2, 4 * (b % 2)
-        X[0, p, r:r + 3, :] = pos[b]
-        V[p, r:r + 3, :] = vel[b]
+        for c in range(3):
+            X[0, p, r + c:r + c + 1, :] = pos[c, b:b + 1, :]
+            V[p, r + c:r + c + 1, :] = vel[c, b:b + 1, :]
     prm[...] = jnp.zeros_like(prm)
     for t in range(2):
         lanes = slice(t * PA, (t + 1) * PA)
@@ -214,16 +251,42 @@
         second = jnp.where(low_rows, pltpu.roll(tile, 4, 0), 0.0)
         return first, second
 
-    def near_block(p, t, q):
-        sources, weighted = nST[p, q], nXS[p, q]
-        first = block_sums(sources, weighted, nT[p, t, 0], 1)
-        second = block_sums(sources, weighted, nT[p, t, 1], 1)
-        both = jnp.where(low_rows, first[:8] + first[8:], second[:8] + second[8:])
-        nG[p, t] += both
-
-    def far_block(t, q):
-        sums = block_sums(fST[q], fXS[q], fT[t], 2)
-        fG[t] += sums[:8] + sums[8:]
+    def near_items(p, part, blocks):
+        items = []
+        for t, q, kind in blocks:
+            others = nXS.at[p, 1] if kind == "cross" else None
+            items += block_items(nST.at[p, q], nXS.at[p, q], nT.at[p, t, part], t, kind, others)
+        return items
+
+    def near_blocks(p, blocks, first):
+        sums = ({}, {})
+        for part in range(2):
+            run_items(near_items(p, part, blocks), 1, sums[part])
+        for t, half in sums[0]:
+            lanes = slice(half * HALF, (half + 1) * HALF)
+            both = jnp.where(rows_of(HALF) < 4, sums[0][t, half], sums[1][t, half])
+            if first:
+                nG[p, t, :, lanes] = both
+            else:
+                nG[p, t, :, lanes] += both
+
+    def far_blocks(blocks, first):
+        items, sums = [], {}
+        for t, q, kind in blocks:
+            others = fXS.at[2] if kind == "cross" else None
+            items += block_items(fST.at[q], fXS.at[q], fT.at[t], t, kind, others)
+        run_items(items, 2, sums)
+        for t, half in sums:
+            lanes = slice(half * HALF, (half + 1) * HALF)
+            if first:
+                fG[t, :, lanes] = sums[t, half]
+            else:
+                fG[t, :, lanes] += sums[t, half]
+
+    near_own = ((0, 1, "self"), (0, 2, "cross"), (1, 2, "self"))
+    near_rim = ((0, 0, "rim"), (1, 3, "rim"))
+    far_own = ((0, 2, "self"), (0, 3, "cross"), (1, 3, "self"))
+    far_rim = ((0, 0, "rim"), (0, 1, "rim"), (0, 4, "rim"), (1, 1, "rim"), (1, 4, "rim"), (1, 5, "rim"))
 
     def phase(k, carry):
         slow_turn = lax.rem(k, INNER_STEPS) == 0
@@ -249,18 +312,15 @@
                 groups = target_features(z)
                 nT[p, t, 0] = masked(groups, 0)
                 nT[p, t, 1] = masked(groups, 1)
-        nG[...] = jnp.zeros_like(nG)
-
-        @pl.loop(0, pairs * 2)
-        def _(n):
-            p, t = n // 2, lax.rem(n, 2)
-            near_block(p, t, 1)
-            near_block(p, t, 2)
 
         @pl.when(k == 0)
         def _():
             for copy in prm_copies:
                 copy.wait_recv()
+
+        @pl.loop(0, pairs // 2)
+        def _(p):
+            near_blocks(p, near_own, True)
 
         @pl.when(slow_turn)
         def _():
@@ -271,18 +331,34 @@
             Y[e] = total
             for copy in y_copies(e):
                 copy.start()
-            for t, half in enumerate(far_halves(total)):
+
+        @pl.loop(pairs // 2, pairs)
+        def _(p):
+            near_blocks(p, near_own, True)
+
+        @pl.when(slow_turn)
+        def _():
+            for t, half in enumerate(far_halves(Y[e])):
                 z = scaled(half, centre, far_rate)
                 z = jnp.where(low_rows, z, 0.0)
                 fST[2 + t], fXS[2 + t] = source_features(z, chg[:, t * PA:(t + 1) * PA])
                 fT[t] = masked(target_features(z), 0)
-            fG[...] = jnp.zeros_like(fG)
-
-            @pl.loop(0, 2)
-            def _(t):
-                far_block(t, 2)
-                far_block(t, 3)
-
+            far_blocks(far_own, True)
+
+        for copy in halo_copies(k):
+            copy.wait_recv()
+        for p in range(pairs):
+            z = scaled(halo_l[k, p], centre_l, near_rate)
+            nST[p, 0], nXS[p, 0] = source_features(z, prm_l[1:2, :])
+            z = scaled(halo_r[k, p], centre_r, near_rate)
+            nST[p, 3], nXS[p, 3] = source_features(z, prm_r[0:1, :])
+
+        @pl.loop(0, pairs)
+        def _(p):
+            near_blocks(p, near_rim, False)
+
+        @pl.when(slow_turn)
+        def _():
             for copy in y_copies(e):
                 copy.wait_recv()
             for base, tile, shares, middle in ((0, y_l, prm_l, centre_l), (4, y_r, prm_r, centre_r)):
@@ -290,35 +366,16 @@
                     z = scaled(half, middle, far_rate)
                     z = jnp.where(low_rows, z, 0.0)
                     fST[base + t], fXS[base + t] = source_features(z, shares[2 + t:3 + t, :])
-
-            @pl.loop(0, 2)
-            def _(t):
-                far_block(t, 1)
-                far_block(t, 4)
-                far_block(t, 5 * t)
-
+            far_blocks(far_rim, False)
             halves = []
-            for t in range(2):
+            for t, half in enumerate(far_halves(Y[e])):
                 lanes = slice(t * PA, (t + 1) * PA)
-                z = scaled(far_halves(total)[t], centre, far_rate)
+                z = scaled(half, centre, far_rate)
                 coefficient = chg[:, lanes] * (far_scale / far_rate)
                 halves.append(coefficient * forces_of(z, fG[t]))
             far_s[e] = jnp.where(low_rows, halves[0], pltpu.roll(halves[1], 4, 0))
             for copy in far_copies(e):
                 copy.start()
-
-        for copy in halo_copies(k):
-            copy.wait_recv()
-        for p in range(pairs):
-            z = scaled(halo_l[k, p], centre_l, near_rate)
-            nST[p, 0], nXS[p, 0] = source_features(z, prm_l[1:2, :])
-            z = scaled(halo_r[k, p], centre_r, near_rate)
-            nST[p, 3], nXS[p, 3] = source_features(z, prm_r[0:1, :])
-
-        @pl.loop(0, pairs)
-        def _(p):
-            near_block(p, 0, 0)
-            near_block(p, 1, 3)
 
         for copy in ring_copies(k):
             copy.wait_recv()
@@ -376,8 +433,9 @@
     last = PHASES - 1
     for b in range(beads_here):
         p, r = b // 2, 4 * (b % 2)
-        moved[b] = X[last, p, r:r + 3, :] - pos[b]
-        final[b] = V[p, r:r + 3, :]
+        for c in range(3):
+            moved[c, b:b + 1, :] = X[last, p, r + c:r + c + 1, :] - pos[c, b:b + 1, :]
+            final[c, b:b + 1, :] = V[p, r + c:r + c + 1, :]
 
     for copy in prm_copies:
         copy.wait_send()
@@ -402,14 +460,14 @@
         pairs = beads_here // 2
         table = jnp.asarray(contraction(beads_here * nb, nb))
         vmem = pl.BlockSpec(memory_space=pltpu.VMEM)
-        out = jax.ShapeDtypeStruct(positions.shape, F32)
+        out = jax.ShapeDtypeStruct((3, beads_here, atoms), F32)
         V, D = pltpu.VMEM, pltpu.SemaphoreType.DMA
         tile = (8, PA)
 
         def body(*refs):
             kernel(nb, ns, 2 * ns, *refs)
 
-        return pl.pallas_call(
+        shifted, speeds = pl.pallas_call(
             body,
             name="rod",
             out_shape=(out, out),
@@ -435,7 +493,8 @@
                 D((EVENTS, nb)), D((EVENTS, nb)),
             ],
             compiler_params=pltpu.CompilerParams(collective_id=0, has_side_effects=True),
-        )(table, positions, velocities, masses[None], amplitudes[None], charges[None])
+        )(table, positions.transpose(1, 0, 2), velocities.transpose(1, 0, 2), masses[None], amplitudes[None], charges[None])
+        return shifted.transpose(1, 0, 2), speeds.transpose(1, 0, 2)
 
     both = P("bead", None, "slab")
     return jax.shard_map(

time: 73.4 us -> 67.9 us (0.925)
  Pallas kernels: 68.2 us -> 65 us
  local copies, waits for them, and re-layouts: 4.31 us -> 2.06 us
    pallas_call x1, Pallas kernels: 68.2 us -> 65 us  [shards(): pl.pallas_call(body, name='rod', out_shape=(out, out), in_specs=[pl.Block...]
    pallas_call x2 -> x0, local copies, waits for them, and re-layouts: 2.18 us -> none  [shards(): pl.pallas_call(body, name='rod', out_shape=(out, out), in_specs=[pl.Block...]
    unnamed x6 -> x4, local copies, waits for them, and re-layouts: 2.13 us -> 2.06 us
where the time goes in v1:
time: 67.9 us; the launch traced here: 67.7 us
  Pallas kernels  65 us (96%)
  local copies, waits for them, and re-layouts  2.06 us (3%)
    pallas_call x1, Pallas kernels, shards(): pl.pallas_call(body, name='rod', out_shape=(out, out), in_specs=[pl.Block...  65 us
    unnamed x4, local copies, waits for them, and re-layouts  2.06 us

profile of v1, /device:TPU:0, one launch (start us, length us, event | category | flops | bytes accessed | tf_op | source)
XLA Modules:
  0.0 67.7 jit_solution(4525410992276757884)
XLA Ops:
  0.6 65.0 %rod.1 = (f32[3,4,1024]{2,1,0:T(4,128)}, f32[3,4,1024]{2,1,0:T(4,128)}) custom-call(f32[4,16]{1,0:T(4,128)} %constant.2.clone.refs_0_, f32[3,4,1024]{2,1,0:T(4,128)} %bitcast.7, f32[3,4,1024]{2,1,0:T(4,128)} %bitcast.8, f32[1,1024]{1,0:T(1,128)} %bitcast.11, f32[1,1024]{1,0:T(1,128)} %bitcast.12, f32[1,1024]{1,0:T(1,128)} %bitcast.13), custom_call_target="tpu_custom_call" | custom-call | tf_op jit(solution)/shard_map/rod/pallas_call | solution.py:470
  65.6 0.0 copy-start
  65.6 1.4 %copy.10 = f32[4,3,1024]{2,0,1:T(4,128)} copy(f32[4,3,1024]{2,0,1:T(4,128)} %bitcast.10) | data formatting | bytes 98304
  67.1 0.0 copy-done
  67.1 0.6 copy.11
Async XLA Ops:
  65.6 1.4 %copy-start = (f32[3,4,1024]{2,1,0:T(4,128)S(1)}, f32[3,4,1024]{2,1,0:T(4,128)}, u32[]{:S(2)}) copy-start(f32[3,4,1024]{2,1,0:T(4,128)} %get-tuple-element.5) | copy-start | bytes 147460

commit v2 on v1

--- a/solution.py
+++ b/solution.py
@@ -113,15 +113,15 @@
     return items
 
 
-def run_items(items, pieces, sums):
+def run_items(items, pieces):
     waiting = None
-    for item in list(items) + [None]:
+    for item, sums_of in list(items) + [(None, None)]:
         exponent = None
         if item is not None:
             sources, rows, _, targets, width = item[:5]
             exponent = jnp.dot(sources[rows, :], targets[:, :width], preferred_element_type=F32)
         if waiting is not None:
-            (_, rows, weighted, _, width, t, flips), held = waiting
+            (_, rows, weighted, _, width, t, flips), held, sums = waiting
             weight = jnp.exp2(held)
             direct = weighted_sum(weighted[:, rows], weight, pieces, False)
             for half in range(width // HALF):
@@ -131,7 +131,7 @@
                 shares, depth, key = flips
                 part = weighted_sum(shares[:, :depth], weight[:, :depth], pieces, True)
                 sums[key] = sums[key] + part if key in sums else part
-        waiting = (item, exponent)
+        waiting = (item, exponent, sums_of)
 
 
 def forces_of(z, sums):
@@ -260,8 +260,7 @@
 
     def near_blocks(p, blocks, first):
         sums = ({}, {})
-        for part in range(2):
-            run_items(near_items(p, part, blocks), 1, sums[part])
+        run_items([(item, sums[part]) for part in range(2) for item in near_items(p, part, blocks)], 1)
         for t, half in sums[0]:
             lanes = slice(half * HALF, (half + 1) * HALF)
             both = jnp.where(rows_of(HALF) < 4, sums[0][t, half], sums[1][t, half])
@@ -275,7 +274,7 @@
         for t, q, kind in blocks:
             others = fXS.at[2] if kind == "cross" else None
             items += block_items(fST.at[q], fXS.at[q], fT.at[t], t, kind, others)
-        run_items(items, 2, sums)
+        run_items([(item, sums) for item in items], 2)
         for t, half in sums:
             lanes = slice(half * HALF, (half + 1) * HALF)
             if first:
@@ -353,7 +352,7 @@
             z = scaled(halo_r[k, p], centre_r, near_rate)
             nST[p, 3], nXS[p, 3] = source_features(z, prm_r[0:1, :])
 
-        @pl.loop(0, pairs)
+        @pl.loop(0, pairs // 2)
         def _(p):
             near_blocks(p, near_rim, False)
 
@@ -376,6 +375,10 @@
             far_s[e] = jnp.where(low_rows, halves[0], pltpu.roll(halves[1], 4, 0))
             for copy in far_copies(e):
                 copy.start()
+
+        @pl.loop(pairs // 2, pairs)
+        def _(p):
+            near_blocks(p, near_rim, False)
 
         for copy in ring_copies(k):
             copy.wait_recv()

time: 67.9 us -> 63.3 us (0.932)
  Pallas kernels: 65 us -> 60.4 us
    pallas_call x1, Pallas kernels: 65 us -> 60.4 us  [shards(): pl.pallas_call(body, name='rod', out_shape=(out, out), in_specs=[pl.Block...]
where the time goes in v2:
time: 63.3 us; the launch traced here: 63.1 us
  Pallas kernels  60.4 us (95%)
  local copies, waits for them, and re-layouts  2.06 us (3%)
  between operations  0.65 us (1%)
    pallas_call x1, Pallas kernels, shards(): pl.pallas_call(body, name='rod', out_shape=(out, out), in_specs=[pl.Block...  60.4 us
    unnamed x4, local copies, waits for them, and re-layouts  2.06 us

profile of v2, /device:TPU:0, one launch (start us, length us, event | category | flops | bytes accessed | tf_op | source)
XLA Modules:
  0.0 63.1 jit_solution(16767809816660789020)
XLA Ops:
  0.6 60.4 %rod.1 = (f32[3,4,1024]{2,1,0:T(4,128)}, f32[3,4,1024]{2,1,0:T(4,128)}) custom-call(f32[4,16]{1,0:T(4,128)} %constant.2.clone.refs_0_, f32[3,4,1024]{2,1,0:T(4,128)} %bitcast.7, f32[3,4,1024]{2,1,0:T(4,128)} %bitcast.8, f32[1,1024]{1,0:T(1,128)} %bitcast.11, f32[1,1024]{1,0:T(1,128)} %bitcast.12, f32[1,1024]{1,0:T(1,128)} %bitcast.13), custom_call_target="tpu_custom_call" | custom-call | tf_op jit(solution)/shard_map/rod/pallas_call | solution.py:473
  61.0 0.0 copy-start
  61.0 1.4 %copy.10 = f32[4,3,1024]{2,0,1:T(4,128)} copy(f32[4,3,1024]{2,0,1:T(4,128)} %bitcast.10) | data formatting | bytes 98304
  62.5 0.0 copy-done
  62.5 0.6 copy.11
Async XLA Ops:
  61.0 1.4 %copy-start = (f32[3,4,1024]{2,1,0:T(4,128)S(1)}, f32[3,4,1024]{2,1,0:T(4,128)}, u32[]{:S(2)}) copy-start(f32[3,4,1024]{2,1,0:T(4,128)} %get-tuple-element.5) | copy-start | bytes 147460

commit v3 on v2

--- a/solution.py
+++ b/solution.py
@@ -312,11 +312,6 @@
                 nT[p, t, 0] = masked(groups, 0)
                 nT[p, t, 1] = masked(groups, 1)
 
-        @pl.when(k == 0)
-        def _():
-            for copy in prm_copies:
-                copy.wait_recv()
-
         @pl.loop(0, pairs // 2)
         def _(p):
             near_blocks(p, near_own, True)
@@ -343,6 +338,11 @@
                 fST[2 + t], fXS[2 + t] = source_features(z, chg[:, t * PA:(t + 1) * PA])
                 fT[t] = masked(target_features(z), 0)
             far_blocks(far_own, True)
+
+        @pl.when(k == 0)
+        def _():
+            for copy in prm_copies:
+                copy.wait_recv()
 
         for copy in halo_copies(k):
             copy.wait_recv()

time: 63.3 us -> 60 us (0.948)
  Pallas kernels: 60.4 us -> 57.1 us
    pallas_call x1, Pallas kernels: 60.4 us -> 57.1 us  [shards(): pl.pallas_call(body, name='rod', out_shape=(out, out), in_specs=[pl.Block...]
where the time goes in v3:
time: 60 us; the launch traced here: 59.8 us
  Pallas kernels  57.1 us (95%)
  local copies, waits for them, and re-layouts  2.06 us (3%)
  between operations  0.65 us (1%)
    pallas_call x1, Pallas kernels, shards(): pl.pallas_call(body, name='rod', out_shape=(out, out), in_specs=[pl.Block...  57.1 us
    unnamed x4, local copies, waits for them, and re-layouts  2.06 us

profile of v3, /device:TPU:0, one launch (start us, length us, event | category | flops | bytes accessed | tf_op | source)
XLA Modules:
  0.0 59.8 jit_solution(3587543713005908524)
XLA Ops:
  0.6 57.1 %rod.1 = (f32[3,4,1024]{2,1,0:T(4,128)}, f32[3,4,1024]{2,1,0:T(4,128)}) custom-call(f32[4,16]{1,0:T(4,128)} %constant.2.clone.refs_0_, f32[3,4,1024]{2,1,0:T(4,128)} %bitcast.7, f32[3,4,1024]{2,1,0:T(4,128)} %bitcast.8, f32[1,1024]{1,0:T(1,128)} %bitcast.11, f32[1,1024]{1,0:T(1,128)} %bitcast.12, f32[1,1024]{1,0:T(1,128)} %bitcast.13), custom_call_target="tpu_custom_call" | custom-call | tf_op jit(solution)/shard_map/rod/pallas_call | solution.py:473
  57.7 0.0 copy-start
  57.7 1.4 %copy.10 = f32[4,3,1024]{2,0,1:T(4,128)} copy(f32[4,3,1024]{2,0,1:T(4,128)} %bitcast.10) | data formatting | bytes 98304
  59.2 0.0 copy-done
  59.2 0.6 %copy.11 = f32[4,3,1024]{2,0,1:T(4,128)} copy(f32[4,3,1024]{2,0,1:T(4,128)S(1)} %bitcast.9) | data formatting | bytes 98304
Async XLA Ops:
  57.7 1.4 %copy-start = (f32[3,4,1024]{2,1,0:T(4,128)S(1)}, f32[3,4,1024]{2,1,0:T(4,128)}, u32[]{:S(2)}) copy-start(f32[3,4,1024]{2,1,0:T(4,128)} %get-tuple-element.5) | copy-start | bytes 147460
